TPU v7x, 256 devices: a whole 4x4x8 slice. The times are simulated.
256 devices in a mesh: pre: 16 (over x_lo, z), tp: 8 (over x_hi, y), dec: 2 (over core).
Axes of the slice: x: 4 (x_hi: 2, x_lo: 2; x = x_hi * 2 + x_lo), y: 4, z: 8, core: 2. Of those that a mesh axis runs over, the one named last changes fastest.
Arguments:
- tokens: bfloat16 [16384, 2048], P(('pre', 'tp', 'dec')), may hold values from -6 to 6
- route_ids: int32 [16384, 6], P(('pre', 'tp', 'dec')), may hold values from 0 to 63, all different within a row; in each aligned block of 64 rows (0 to 63, 64 to 127, ...) at most 12 rows name the same one
- route_weights: float32 [16384, 6], P(('pre', 'tp', 'dec')), may hold values from 0.05 to 0.4
- gate_weight: bfloat16 [2048, 90112], P(None, ('pre', 'tp')), may hold values from -0.125 to 0.125
- up_weight: bfloat16 [2048, 90112], P(None, ('pre', 'tp')), may hold values from -0.125 to 0.125
- down_weight: bfloat16 [90112, 2048], P(('pre', 'tp')), may hold values from -0.15625 to 0.15625
- prefill_cache: bfloat16 [2, 8, 256, 64, 1024], P(None, 'tp', 'pre', None, 'dec'), may hold values from -6 to 6
- handover_table: int32 [8, 256], replicated, may hold values from 0 to 255, as said below
Outputs:
- moe_output: bfloat16 [16384, 2048], P(('pre', 'tp', 'dec'))
- decode_cache: bfloat16 [2, 8, 256, 64, 1024], P(None, 'tp', 'pre', None, 'dec')
Inputs may be any that keep to these rules, and one draw needn't show every extreme that they name: `route_ids`: each token names 6 different experts; within the rows of one device (64 consecutive tokens) no expert is named by more than 12 routes, a bound that some block reaches. `handover_table`: each row is a permutation of 0 to 255. The 16 slots g with g // 16 = s (one prefill device) map to at most 2 slots q with q // 16 = p (one decode device), for every s and p, and to exactly 2 for some pair.
All inputs are finite; a program needn't handle non-finite values.
Results may differ from a plain program's by a relative error of at most 0.0085.
Values may be sent and summed in bfloat16 or wider, within the bound.
No kernel may reach another device: no remote copies, remote signals or barrier semaphores. Data moves between devices by JAX's collectives and lax.ppermute only.
A program may use at most 128 MiB of HBM per device.

v0:
```python
import jax
import jax.numpy as jnp
from jax import lax
from jax.sharding import PartitionSpec as P


def slot_ranks(labels, count):
    onehot = (labels[:, None] == jnp.arange(count, dtype=jnp.int32)[None, :]).astype(jnp.int32)
    before = jnp.cumsum(onehot, axis=0) - onehot
    return jnp.sum(before * onehot, axis=1)


def shards(
    tokens,
    route_ids,
    route_weights,
    gate_weight,
    up_weight,
    down_weight,
    prefill_cache,
    handover_table,
):
    tok_dev, width = tokens.shape
    top_count = route_ids.shape[1]
    groups = lax.axis_size("pre") * lax.axis_size("tp")
    experts_all = groups // 2
    most = min(tok_dev, 2 * tok_dev * top_count // experts_all)
    ids_flat = route_ids.reshape(-1)
    positions = slot_ranks(ids_flat, experts_all)
    dest_row = ids_flat * most + positions
    source_rows = jnp.repeat(jnp.arange(tok_dev, dtype=jnp.int32), top_count)
    packed = (
        jnp.zeros((experts_all * most, width), jnp.bfloat16).at[dest_row].set(tokens[source_rows])
    )
    outgoing = jnp.broadcast_to(
        packed.reshape(experts_all, 1, most, width), (experts_all, 2, most, width)
    )
    outgoing = outgoing.reshape(groups, most, width)
    received = lax.all_to_all(outgoing, ("pre", "tp"), split_axis=0, concat_axis=0, tiled=True)
    flat = received.reshape(-1, width)
    gate = jnp.dot(flat, gate_weight, preferred_element_type=jnp.float32)
    upper = jnp.dot(flat, up_weight, preferred_element_type=jnp.float32)
    hidden = (jax.nn.silu(gate) * upper).astype(jnp.bfloat16)
    result = jnp.dot(hidden, down_weight, preferred_element_type=jnp.float32)
    partial_out = result.reshape(received.shape[0], received.shape[1], width)
    returned = lax.all_to_all(partial_out, ("pre", "tp"), split_axis=0, concat_axis=0, tiled=True)
    expert_rows = jnp.sum(returned.reshape(experts_all, 2, most, width), axis=1).astype(
        jnp.bfloat16
    )
    picked = expert_rows.reshape(-1, width)[dest_row].reshape(tok_dev, top_count, width)
    moe_output = jnp.einsum("tk,tkd->td", route_weights, picked.astype(jnp.float32)).astype(
        jnp.bfloat16
    )
    layers, _, blk_dev, blk, half_width = prefill_cache.shape
    sources = lax.axis_size("pre")
    spare = blk_dev // sources + 1
    column = lax.dynamic_index_in_dim(handover_table, lax.axis_index("tp"), 0, keepdims=False)
    dest_dev = (column // blk_dev).reshape(sources, blk_dev)
    onehot = (dest_dev[:, :, None] == jnp.arange(sources, dtype=jnp.int32)[None, None, :]).astype(
        jnp.int32
    )
    rank_all = jnp.sum((jnp.cumsum(onehot, axis=1) - onehot) * onehot, axis=2)
    here = lax.axis_index("pre")
    my_dest = lax.dynamic_index_in_dim(dest_dev, here, 0, keepdims=False)
    my_rank = lax.dynamic_index_in_dim(rank_all, here, 0, keepdims=False)
    blocks_out = jnp.zeros((layers, sources, spare, blk, half_width), jnp.bfloat16)
    blocks_out = blocks_out.at[:, my_dest, my_rank].set(prefill_cache[:, 0])
    arrived = lax.all_to_all(blocks_out, "pre", split_axis=1, concat_axis=1, tiled=True)
    pool_size = column.shape[0]
    inverse = (
        jnp.zeros((pool_size,), jnp.int32).at[column].set(jnp.arange(pool_size, dtype=jnp.int32))
    )
    anchor = lax.dynamic_slice_in_dim(inverse, here * blk_dev, blk_dev)
    pick = anchor // blk_dev * spare + rank_all.reshape(-1)[anchor]
    decode_cache = arrived.reshape(layers, sources * spare, blk, half_width)[:, pick][:, None]
    return (moe_output, decode_cache)


def solution(mesh):
    return jax.shard_map(
        shards,
        mesh=mesh,
        in_specs=(
            P(("pre", "tp", "dec"), None),
            P(("pre", "tp", "dec"), None),
            P(("pre", "tp", "dec"), None),
            P(None, ("pre", "tp")),
            P(None, ("pre", "tp")),
            P(("pre", "tp"), None),
            P(None, "tp", "pre", None, "dec"),
            P(),
        ),
        out_specs=(P(("pre", "tp", "dec"), None), P(None, "tp", "pre", None, "dec")),
        check_vma=False,
    )
```

profile of v0, /device:TPU:96, one launch (start us, length us, event | category | flops | bytes accessed | tf_op | source)
XLA Modules:
  0.0 748.9 jit_solution(11944358911356710262)
XLA Ops:
  0.6 0.0 copy-start
  0.6 0.8 broadcast_multiply_fusion
  1.5 0.8 copy.28
  2.3 0.1 eq.38
  2.4 0.1 eq.42
  2.6 0.1 copy.27
  2.7 0.1 mul.37
  2.8 0.9 reduce-window.6
  3.7 0.2 slice_reduce_fusion
  4.0 0.1 reshape.222
  4.2 0.1 fusion.8
  4.3 10.4 %scatter_custom_fusion = bf16[768,2048]{1,0:T(8,128)(2,1)} fusion(s32[384]{0:T(512)S(1)} %fusion.13, bf16[64,2048]{1,0:T(8,128)(2,1)} %param.8, s32[1024]{0:T(1024)S(1)} %pad_clamp_fusion.3, bf16[]{:T(256)} %constant.63.clone.1), kind=kCustom, calls=%fused_computation.9 | custom fusion | bytes 3146240 | tf_op jit(solution)/shard_map/scatter | solution.py:33
  14.7 6.1 broadcast_in_dim.35
  20.8 6.7 broadcast_in_dim.36
  27.5 14.6 %all-to-all-start = ((bf16[128,12,2048]{2,1,0:T(8,128)(2,1)}), bf16[128,12,2048]{2,1,0:T(8,128)(2,1)}, u32[]{:S(2)}, u32[]{:S(2)}) async-start(bf16[128,12,2048]{2,1,0:T(8,128)(2,1)} %bitcast.56), calls=%async_computation | async-start | bytes 16777216 | tf_op jit(solution)/shard_map/all_to_all | solution.py:39
  42.1 0.7 fusion.20
  42.9 0.1 squeeze.16
  42.9 0.1 copy.31
  43.0 3.1 copy.32
  46.2 0.5 fusion.22
  46.6 0.2 dynamic-slice_reduce_fusion
  46.8 2.4 broadcast_in_dim.37
  49.3 6.0 scatter_fusion
  55.3 4.6 copy.33
  59.9 168.8 %all-to-all-done = bf16[128,12,2048]{2,1,0:T(8,128)(2,1)} async-done(((bf16[128,12,2048]{2,1,0:T(8,128)(2,1)}), bf16[128,12,2048]{2,1,0:T(8,128)(2,1)}, u32[]{:S(2)}, u32[]{:S(2)}) %all-to-all-start) | async-done | bytes 6291488 | tf_op jit(solution)/shard_map/all_to_all | solution.py:39
  228.8 5.7 all-to-all-start.2
  234.5 10.7 %reshape.224 = bf16[1536,2048]{1,0:T(8,128)(2,1)} reshape(bf16[128,12,2048]{2,1,0:T(8,128)(2,1)} %all-to-all-done) | data formatting | bytes 12582912 | tf_op jit(solution)/shard_map/reshape | solution.py:40
  245.2 10.3 %fusion.23 = f32[1536,704]{0,1:T(8,128)} fusion(bf16[1536,2048]{1,0:T(8,128)(2,1)} %reshape.224, bf16[2048,704]{0,1:T(8,128)(2,1)} %param.11), kind=kOutput, calls=%fused_computation.67 | convolution fusion | flops 4429185024 | bytes 13500416 | tf_op jit(solution)/shard_map/dot_general | solution.py:41
  255.5 0.0 copy-done
  255.5 19.1 %fusion.4 = f32[1536,2048]{1,0:T(8,128)} fusion(bf16[704,2048]{1,0:T(8,128)(2,1)S(1)} %copy-done, f32[1536,704]{0,1:T(8,128)} %fusion.23, bf16[1536,2048]{1,0:T(8,128)(2,1)} %reshape.224, bf16[2048,704]{0,1:T(8,128)(2,1)} %param.12), kind=kOutput, calls=%fused_computation.14 | convolution fusion | flops 8864858112 | bytes 28966912 | tf_op jit(solution)/shard_map/dot_general | solution.py:44
  274.6 14.9 %reshape.225 = f32[128,12,2048]{2,1,0:T(8,128)} reshape(f32[1536,2048]{1,0:T(8,128)} %fusion.4) | data formatting | bytes 25165824 | tf_op jit(solution)/shard_map/reshape | solution.py:45
  289.5 0.0 copy-start.2
  289.5 38.4 %all-to-all-done.2 = bf16[2,16,2,64,512]{4,3,2,0,1:T(8,128)(2,1)} async-done(((bf16[2,16,2,64,512]{4,3,2,0,1:T(8,128)(2,1)}), bf16[2,16,2,64,512]{4,3,2,0,1:T(8,128)(2,1)}, u32[]{:S(2)}, u32[]{:S(2)}) %all-to-all-start.2) | async-done | bytes 4194336 | tf_op jit(solution)/shard_map/all_to_all | solution.py:68
  327.9 13.0 %all-to-all-start.1 = ((f32[128,12,2048]{2,1,0:T(8,128)}), f32[128,12,2048]{2,1,0:T(8,128)}, u32[]{:S(2)}, u32[]{:S(2)}) async-start(f32[128,12,2048]{2,1,0:T(8,128)} %reshape.225), calls=%async_computation.1 | async-start | bytes 33554432 | tf_op jit(solution)/shard_map/all_to_all | solution.py:46
  340.9 0.1 copy.35
  341.0 0.0 copy-done.2
  341.0 0.1 copy.37
  341.1 0.1 reshape.229
  341.2 0.7 compare_select_fusion.2
  341.9 1.4 scatter_custom_fusion.2
  343.3 0.1 compare_select_fusion.6
  343.4 0.7 gather_fusion.1
  344.1 0.1 compare_select_fusion.3
  344.2 4.6 copy.34
  348.8 2.9 gather_fusion.2
  351.7 1.5 copy.36
  353.2 365.6 %all-to-all-done.1 = f32[128,12,2048]{2,1,0:T(8,128)} async-done(((f32[128,12,2048]{2,1,0:T(8,128)}), f32[128,12,2048]{2,1,0:T(8,128)}, u32[]{:S(2)}, u32[]{:S(2)}) %all-to-all-start.1) | async-done | bytes 12582944 | tf_op jit(solution)/shard_map/all_to_all | solution.py:46
  718.8 9.6 %bitcast_reduce_fusion = bf16[64,12,2048]{2,1,0:T(8,128)(2,1)} fusion(f32[128,12,2048]{2,1,0:T(8,128)} %all-to-all-done.1), kind=kLoop, calls=%fused_computation.7 | loop fusion | flops 1572864 | bytes 15728640 | tf_op jit(solution)/shard_map/reduce_sum | solution.py:47
  728.4 6.2 convert_element_type.28
  734.5 0.0 copy-start.1
  734.5 7.5 %gather_fusion = bf16[384,2048]{1,0:T(8,128)(2,1)} fusion(bf16[768,2048]{1,0:T(8,128)(2,1)} %convert_element_type.28, s32[1024]{0:T(1024)S(1)} %pad_clamp_fusion.2), kind=kCustom, calls=%fused_computation.1 | custom fusion | bytes 3147264 | tf_op jit(solution)/shard_map/gather | solution.py:50
  742.0 3.7 reshape.227
  745.7 2.3 fusion.24
  748.0 0.9 copy.42
  748.9 0.0 copy-done.1
  (12 shorter events, 0.2 us)
Async XLA Ops:
  0.6 254.8 %copy-start = (bf16[704,2048]{1,0:T(8,128)(2,1)S(1)}, bf16[704,2048]{1,0:T(8,128)(2,1)}, u32[]{:S(2)}) copy-start(bf16[704,2048]{1,0:T(8,128)(2,1)} %param.13) | copy-start | bytes 8650756
  27.5 201.3 %all-to-all-start = ((bf16[128,12,2048]{2,1,0:T(8,128)(2,1)}), bf16[128,12,2048]{2,1,0:T(8,128)(2,1)}, u32[]{:S(2)}, u32[]{:S(2)}) async-start(bf16[128,12,2048]{2,1,0:T(8,128)(2,1)} %bitcast.56), calls=%async_computation | async-start | bytes 16777216 | tf_op jit(solution)/shard_map/all_to_all | solution.py:39
  228.8 99.1 %all-to-all-start.2 = ((bf16[2,16,2,64,512]{4,3,2,0,1:T(8,128)(2,1)}), bf16[2,16,2,64,512]{4,3,2,0,1:T(8,128)(2,1)}, u32[]{:S(2)}, u32[]{:S(2)}) async-start(bf16[2,16,2,64,512]{4,3,2,0,1:T(8,128)(2,1)} %copy.33), calls=%async_computation.2 | async-start | bytes 8388608 | tf_op jit(solution)/shard_map/all_to_all | solution.py:68
  289.5 51.5 %copy-start.2 = (f32[64,6]{0,1:T(8,128)S(1)}, f32[64,6]{0,1:T(8,128)}, u32[]{:S(2)}) copy-start(f32[64,6]{0,1:T(8,128)} %param.10) | copy-start | bytes 4612
  327.9 390.9 %all-to-all-start.1 = ((f32[128,12,2048]{2,1,0:T(8,128)}), f32[128,12,2048]{2,1,0:T(8,128)}, u32[]{:S(2)}, u32[]{:S(2)}) async-start(f32[128,12,2048]{2,1,0:T(8,128)} %reshape.225), calls=%async_computation.1 | async-start | bytes 33554432 | tf_op jit(solution)/shard_map/all_to_all | solution.py:46
  734.5 14.3 %copy-start.1 = (bf16[704,2048]{1,0:T(8,128)(2,1)S(1)}, bf16[704,2048]{1,0:T(8,128)(2,1)}, u32[]{:S(2)}) copy-start(bf16[704,2048]{1,0:T(8,128)(2,1)} %param.13) | copy-start | bytes 8650756
where the time goes:
time: 751 us; the launch traced here: 749 us
  waiting for transfers between devices  573 us (76%)
  local copies, waits for them, and re-layouts  97.3 us (13%)
  starting transfers between devices  33.4 us (4%)
  matrix products  31.7 us (4%)
  other arithmetic  12.9 us (2%)
    all_to_all x1, waiting for transfers between devices, shards(): lax.all_to_all(partial_out, ('pre', 'tp'), split_axis=0, concat_axis=0, t...  366 us
    all_to_all x1, waiting for transfers between devices, shards(): lax.all_to_all(outgoing, ('pre', 'tp'), split_axis=0, concat_axis=0, tile...  169 us
    all_to_all x1, waiting for transfers between devices, shards(): lax.all_to_all(blocks_out, 'pre', split_axis=1, concat_axis=1, tiled=True)  38.4 us
    dot_general x1, matrix products, shards(): result = jnp.dot(hidden, down_weight, preferred_element_type=jnp.float32)  19.1 us
  transfers between devices with their start and end apart: 3, of which 3 were waited for; matrix products, arithmetic and copies ran while one was open for 11% of the time, Pallas kernels for 0%

commit v1 on v0

--- a/solution.py
+++ b/solution.py
@@ -65,7 +65,10 @@
     my_rank = lax.dynamic_index_in_dim(rank_all, here, 0, keepdims=False)
     blocks_out = jnp.zeros((layers, sources, spare, blk, half_width), jnp.bfloat16)
     blocks_out = blocks_out.at[:, my_dest, my_rank].set(prefill_cache[:, 0])
-    arrived = lax.all_to_all(blocks_out, "pre", split_axis=1, concat_axis=1, tiled=True)
+    arrived = jnp.concatenate(
+        lax.all_to_all(jnp.stack(jnp.split(blocks_out, lax.axis_size("pre"), axis=1)), "pre", 0, 0),
+        axis=1,
+    )
     pool_size = column.shape[0]
     inverse = (
         jnp.zeros((pool_size,), jnp.int32).at[column].set(jnp.arange(pool_size, dtype=jnp.int32))

time: 751 us -> 751 us (level)
  waiting for transfers between devices: 573 us -> 551 us
  local copies, waits for them, and re-layouts: 97.3 us -> 119 us
    unnamed x9 -> x24, local copies, waits for them, and re-layouts: 2.48 us -> 27.6 us
    all_to_all x1, waiting for transfers between devices: 169 us -> 147 us  [shards(): lax.all_to_all(outgoing, ('pre', 'tp'), split_axis=0, concat_axis=0, tile...]
  transfers between devices with their start and end apart: 3 -> 3, of which waited for: 3 -> 3; matrix products, arithmetic and copies ran while one was open for 11% -> 14% of each run, Pallas kernels for 0% -> 0%
where the time goes in v1:
time: 751 us; the launch traced here: 749 us
  waiting for transfers between devices  551 us (73%)
  local copies, waits for them, and re-layouts  119 us (16%)
  starting transfers between devices  33.4 us (4%)
  matrix products  31.7 us (4%)
  other arithmetic  12.9 us (2%)
    all_to_all x1, waiting for transfers between devices, shards(): lax.all_to_all(partial_out, ('pre', 'tp'), split_axis=0, concat_axis=0, t...  366 us
    all_to_all x1, waiting for transfers between devices, shards(): lax.all_to_all(outgoing, ('pre', 'tp'), split_axis=0, concat_axis=0, tile...  147 us
    all_to_all x1, waiting for transfers between devices, shards(): lax.all_to_all(jnp.stack(jnp.split(blocks_out, lax.axis_size('pre'), axis...  38.4 us
    unnamed x24, local copies, waits for them, and re-layouts  27.6 us
    dot_general x1, matrix products, shards(): result = jnp.dot(hidden, down_weight, preferred_element_type=jnp.float32)  19.1 us
  transfers between devices with their start and end apart: 3, of which 3 were waited for; matrix products, arithmetic and copies ran while one was open for 14% of the time, Pallas kernels for 0%

profile of v1, /device:TPU:96, one launch (start us, length us, event | category | flops | bytes accessed | tf_op | source)
XLA Modules:
  0.0 748.9 jit_solution(7959480846501764847)
XLA Ops:
  0.6 0.8 broadcast_multiply_fusion
  1.5 0.8 copy.73
  2.3 0.1 eq.38
  2.4 0.1 eq.42
  2.6 0.1 copy.72
  2.7 0.1 mul.37
  2.8 0.9 reduce-window.6
  3.7 0.2 slice_reduce_fusion
  4.0 0.1 reshape.222
  4.2 0.1 fusion.24
  4.3 10.4 %scatter_custom_fusion = bf16[768,2048]{1,0:T(8,128)(2,1)} fusion(s32[384]{0:T(512)S(1)} %fusion.29, bf16[64,2048]{1,0:T(8,128)(2,1)} %param.8, s32[1024]{0:T(1024)S(1)} %pad_clamp_fusion.3, bf16[]{:T(256)} %constant.63.clone.1), kind=kCustom, calls=%fused_computation.9 | custom fusion | bytes 3146240 | tf_op jit(solution)/shard_map/scatter | solution.py:33
  14.7 6.1 broadcast_in_dim.35
  20.8 6.7 broadcast_in_dim.36
  27.5 14.6 %all-to-all-start = ((bf16[128,12,2048]{2,1,0:T(8,128)(2,1)}), bf16[128,12,2048]{2,1,0:T(8,128)(2,1)}, u32[]{:S(2)}, u32[]{:S(2)}) async-start(bf16[128,12,2048]{2,1,0:T(8,128)(2,1)} %bitcast.151), calls=%async_computation | async-start | bytes 16777216 | tf_op jit(solution)/shard_map/all_to_all | solution.py:39
  42.1 0.7 fusion.36
  42.9 0.1 squeeze.16
  42.9 0.1 copy.76
  43.0 3.1 copy.77
  46.2 0.5 fusion.38
  46.6 0.2 dynamic-slice_reduce_fusion
  46.8 2.4 broadcast_in_dim.37
  49.3 6.0 scatter_fusion
  55.3 1.7 fusion.20
  57.0 1.7 fusion.19
  58.7 1.7 fusion.18
  60.3 1.7 fusion.17
  62.0 1.7 fusion.16
  63.7 1.7 fusion.15
  65.3 1.7 fusion.14
  67.0 1.7 fusion.13
  68.7 1.7 fusion.12
  70.3 1.7 fusion.11
  72.0 1.7 fusion.10
  73.7 1.7 fusion.9
  75.4 1.7 fusion.8
  77.0 1.7 fusion.7
  78.7 1.7 fusion.6
  80.4 1.7 fusion.5
  82.1 146.7 %all-to-all-done = bf16[128,12,2048]{2,1,0:T(8,128)(2,1)} async-done(((bf16[128,12,2048]{2,1,0:T(8,128)(2,1)}), bf16[128,12,2048]{2,1,0:T(8,128)(2,1)}, u32[]{:S(2)}, u32[]{:S(2)}) %all-to-all-start) | async-done | bytes 6291488 | tf_op jit(solution)/shard_map/all_to_all | solution.py:39
  228.8 5.7 all-to-all-start.2
  234.5 10.7 %reshape.224 = bf16[1536,2048]{1,0:T(8,128)(2,1)} reshape(bf16[128,12,2048]{2,1,0:T(8,128)(2,1)} %all-to-all-done) | data formatting | bytes 12582912 | tf_op jit(solution)/shard_map/reshape | solution.py:40
  245.2 10.3 %fusion.39 = f32[1536,704]{0,1:T(8,128)} fusion(bf16[1536,2048]{1,0:T(8,128)(2,1)} %reshape.224, bf16[2048,704]{0,1:T(8,128)(2,1)} %param.11), kind=kOutput, calls=%fused_computation.99 | convolution fusion | flops 4429185024 | bytes 13500416 | tf_op jit(solution)/shard_map/dot_general | solution.py:41
  255.5 19.1 %fusion.4 = f32[1536,2048]{1,0:T(8,128)} fusion(bf16[704,2048]{1,0:T(8,128)(2,1)S(1)} %copy-done, f32[1536,704]{0,1:T(8,128)} %fusion.39, bf16[1536,2048]{1,0:T(8,128)(2,1)} %reshape.224, bf16[2048,704]{0,1:T(8,128)(2,1)} %param.12), kind=kOutput, calls=%fused_computation.14 | convolution fusion | flops 8864858112 | bytes 28966912 | tf_op jit(solution)/shard_map/dot_general | solution.py:44
  274.6 14.9 %reshape.225 = f32[128,12,2048]{2,1,0:T(8,128)} reshape(f32[1536,2048]{1,0:T(8,128)} %fusion.4) | data formatting | bytes 25165824 | tf_op jit(solution)/shard_map/reshape | solution.py:45
  289.5 38.4 %all-to-all-done.2 = bf16[16,2,1,2,64,512]{5,4,3,1,2,0:T(8,128)(2,1)} async-done(((bf16[16,2,1,2,64,512]{5,4,3,1,2,0:T(8,128)(2,1)}), bf16[16,2,1,2,64,512]{5,4,3,1,2,0:T(8,128)(2,1)}, u32[]{:S(2)}, u32[]{:S(2)}) %all-to-all-start.2) | async-done | bytes 4194336 | tf_op jit(solution)/shard_map/all_to_all | solution.py:69
  327.9 13.0 %all-to-all-start.1 = ((f32[128,12,2048]{2,1,0:T(8,128)}), f32[128,12,2048]{2,1,0:T(8,128)}, u32[]{:S(2)}, u32[]{:S(2)}) async-start(f32[128,12,2048]{2,1,0:T(8,128)} %reshape.225), calls=%async_computation.1 | async-start | bytes 33554432 | tf_op jit(solution)/shard_map/all_to_all | solution.py:46
  340.9 0.1 copy.94
  341.0 0.1 copy.96
  341.1 0.1 reshape.229
  341.2 0.7 compare_select_fusion.2
  341.9 1.4 scatter_custom_fusion.2
  343.3 0.1 compare_select_fusion.6
  343.4 0.7 gather_fusion.1
  344.1 0.1 compare_select_fusion.3
  344.2 4.6 copy.93
  348.8 2.9 gather_fusion.2
  351.7 1.5 copy.95
  353.2 365.6 %all-to-all-done.1 = f32[128,12,2048]{2,1,0:T(8,128)} async-done(((f32[128,12,2048]{2,1,0:T(8,128)}), f32[128,12,2048]{2,1,0:T(8,128)}, u32[]{:S(2)}, u32[]{:S(2)}) %all-to-all-start.1) | async-done | bytes 12582944 | tf_op jit(solution)/shard_map/all_to_all | solution.py:46
  718.8 9.6 %bitcast_reduce_fusion = bf16[64,12,2048]{2,1,0:T(8,128)(2,1)} fusion(f32[128,12,2048]{2,1,0:T(8,128)} %all-to-all-done.1), kind=kLoop, calls=%fused_computation.7 | loop fusion | flops 1572864 | bytes 15728640 | tf_op jit(solution)/shard_map/reduce_sum | solution.py:47
  728.4 6.2 convert_element_type.28
  734.5 7.5 %gather_fusion = bf16[384,2048]{1,0:T(8,128)(2,1)} fusion(bf16[768,2048]{1,0:T(8,128)(2,1)} %convert_element_type.28, s32[1024]{0:T(1024)S(1)} %pad_clamp_fusion.2), kind=kCustom, calls=%fused_computation.1 | custom fusion | bytes 3147264 | tf_op jit(solution)/shard_map/gather | solution.py:50
  742.0 3.7 reshape.227
  745.7 2.3 fusion.40
  748.0 0.9 copy.116
  (18 shorter events, 0.2 us)
Async XLA Ops:
  0.6 254.8 %copy-start = (bf16[704,2048]{1,0:T(8,128)(2,1)S(1)}, bf16[704,2048]{1,0:T(8,128)(2,1)}, u32[]{:S(2)}) copy-start(bf16[704,2048]{1,0:T(8,128)(2,1)} %param.13) | copy-start | bytes 8650756
  27.5 201.3 %all-to-all-start = ((bf16[128,12,2048]{2,1,0:T(8,128)(2,1)}), bf16[128,12,2048]{2,1,0:T(8,128)(2,1)}, u32[]{:S(2)}, u32[]{:S(2)}) async-start(bf16[128,12,2048]{2,1,0:T(8,128)(2,1)} %bitcast.151), calls=%async_computation | async-start | bytes 16777216 | tf_op jit(solution)/shard_map/all_to_all | solution.py:39
  228.8 99.1 %all-to-all-start.2 = ((bf16[16,2,1,2,64,512]{5,4,3,1,2,0:T(8,128)(2,1)}), bf16[16,2,1,2,64,512]{5,4,3,1,2,0:T(8,128)(2,1)}, u32[]{:S(2)}, u32[]{:S(2)}) async-start(bf16[16,2,1,2,64,512]{5,4,3,1,2,0:T(8,128)(2,1)} %fusion.5), calls=%async_computation.2 | async-start | bytes 8388608 | tf_op jit(solution)/shard_map/all_to_all | solution.py:69
  289.5 51.5 %copy-start.2 = (f32[64,6]{0,1:T(8,128)S(1)}, f32[64,6]{0,1:T(8,128)}, u32[]{:S(2)}) copy-start(f32[64,6]{0,1:T(8,128)} %param.10) | copy-start | bytes 4612
  327.9 390.9 %all-to-all-start.1 = ((f32[128,12,2048]{2,1,0:T(8,128)}), f32[128,12,2048]{2,1,0:T(8,128)}, u32[]{:S(2)}, u32[]{:S(2)}) async-start(f32[128,12,2048]{2,1,0:T(8,128)} %reshape.225), calls=%async_computation.1 | async-start | bytes 33554432 | tf_op jit(solution)/shard_map/all_to_all | solution.py:46
  734.5 14.3 %copy-start.1 = (bf16[704,2048]{1,0:T(8,128)(2,1)S(1)}, bf16[704,2048]{1,0:T(8,128)(2,1)}, u32[]{:S(2)}) copy-start(bf16[704,2048]{1,0:T(8,128)(2,1)} %param.13) | copy-start | bytes 8650756
